TPU v7x, 32 devices: a whole 2x2x4 slice. The times are simulated.
32 devices in a mesh: tm: 8 (over z, core), zone: 4 (over y, x).
Axes of the slice: x: 2, y: 2, z: 4, core: 2. Of those that a mesh axis runs over, the one named last changes fastest.
Arguments:
- initial_guess: float32 [15, 3, 4, 1024], P(None, None, 'zone', 'tm'), may hold values from -2.5 to 2.5
- harmonic_loads: float32 [15, 3, 4, 1024], P(None, None, 'zone', 'tm'), may hold values from -12 to 12
- stiffness: bfloat16 [4, 8, 5, 384, 384], P('zone', 'tm'), as said below
- mass_tiles: bfloat16 [4, 8, 384, 384], P('zone', 'tm'), as said below
- block_links: int32 [4, 8, 2], P('zone', 'tm'), may hold values from 0 to 7, as said below
- states: int32 [2048, 4, 1024], P('tm', 'zone'), may hold values from 0 to 2
- preload: float32 [4, 1024], P('zone'), may hold values from 1 to 3
- normal_stiff: float32 [4, 1024], P('zone'), may hold values from 0.5 to 2
- tangent_stiff: float32 [4, 1024], P('zone'), may hold values from 0.3 to 1.5
- friction: float32 [4, 1024], P('zone'), may hold values from 0.2 to 0.8
Outputs:
- coefficients: float32 [15, 3, 4, 1024], P(None, None, 'zone', 'tm')
- residual: float32 [15, 3, 4, 1024], P(None, None, 'zone', 'tm')
Inputs may be any that keep to these rules, and one draw needn't show every extreme that they name: `block_links`: in each row the 2 entries are distinct and differ from the row's own block index (the second index). `stiffness`: in slot 0 every diagonal entry lies between 4 and 8. `mass_tiles`: every diagonal entry lies between 0.5 and 1.
All inputs are finite; a program needn't handle non-finite values.
Results may differ from a plain program's by a relative error of at most 0.0003.
Values sent between devices are 32-bit elements; how exact they have to be, the bound alone decides.
A program may use at most 64 MiB of HBM per device.

v0:
```python
import math
import jax
import jax.numpy as jnp
from jax import lax
from jax.sharding import PartitionSpec as P

DIRS = 3
BLOCK = 128
ITERS = 2
OMEGA_SQUARED = 0.05
SMOOTHING = 0.1
FULL_PRECISION = lax.Precision.HIGHEST


def padded(cells, sides, width):
    for axis, dim in sides:
        count = lax.axis_size(axis)
        head = lax.slice_in_dim(cells, 0, width, axis=dim)
        tail = lax.slice_in_dim(cells, cells.shape[dim] - width, cells.shape[dim], axis=dim)
        cells = jnp.concatenate(
            [
                lax.ppermute(tail, axis, [(i, (i + 1) % count) for i in range(count)]),
                cells,
                lax.ppermute(head, axis, [((i + 1) % count, i) for i in range(count)]),
            ],
            axis=dim,
        )
    return cells


def harmonic_orders(coeff_count):
    row_index = jnp.arange(coeff_count, dtype=jnp.int32)
    return (row_index + 1) // 2


def synthesis_table(first_sample, sample_count, total_samples, coeff_count):
    samples_here = first_sample + jnp.arange(sample_count, dtype=jnp.int32)
    orders = harmonic_orders(coeff_count)
    phases = samples_here[:, None] * orders[None, :] % total_samples
    angles = phases.astype(jnp.float32) * (2.0 * math.pi / total_samples)
    row_index = jnp.arange(coeff_count, dtype=jnp.int32)
    is_sine = (row_index % 2 == 0) & (row_index > 0)
    return jnp.where(is_sine[None, :], jnp.sin(angles), jnp.cos(angles))


def analysis_table(synthesis, coeff_count, total_samples):
    orders = harmonic_orders(coeff_count)
    scaling = jnp.where(orders == 0, 1.0, 2.0) / total_samples
    return synthesis * scaling[None, :]


def contact_law(motion, states, preload, normal_stiff, tangent_stiff, friction):
    normal_part = preload + normal_stiff * motion[:, 0]
    slide_one = motion[:, 1]
    slide_two = motion[:, 2]
    magnitude = jnp.sqrt(slide_one * slide_one + slide_two * slide_two + SMOOTHING * SMOOTHING)
    touching = states > 0
    sticking = states == 1
    normal_force = jnp.where(touching, normal_part, 0.0)
    slip_factor = friction * normal_force / magnitude
    tangent_factor = jnp.where(sticking, tangent_stiff, slip_factor)
    tangent_factor = jnp.where(touching, tangent_factor, 0.0)
    return jnp.stack([normal_force, tangent_factor * slide_one, tangent_factor * slide_two], axis=1)


def block_view(coeff_field):
    coeff_count, direction_count, node_count = coeff_field.shape
    divided = coeff_field.reshape(coeff_count, direction_count, node_count // BLOCK, BLOCK)
    return divided.transpose(2, 0, 1, 3).reshape(
        node_count // BLOCK, coeff_count, direction_count * BLOCK
    )


def field_view(blocks):
    block_count, coeff_count, block_width = blocks.shape
    divided = blocks.reshape(block_count, coeff_count, DIRS, BLOCK)
    return divided.transpose(1, 2, 0, 3).reshape(coeff_count, DIRS, block_count * BLOCK)


def coupled_update(
    own_field, zone_coeffs, sectors, stiffness, mass_tiles, block_links, forces, own_loads
):
    orders = harmonic_orders(own_field.shape[0]).astype(jnp.float32)
    inertia = OMEGA_SQUARED * orders * orders
    own_blocks = block_view(own_field)
    zone_blocks = block_view(zone_coeffs)
    before_blocks = block_view(sectors[:, :, 0, :])
    after_blocks = block_view(sectors[:, :, 2, :])
    linked = zone_blocks[block_links]
    sources = jnp.concatenate(
        [own_blocks[:, None], before_blocks[:, None], after_blocks[:, None], linked], axis=1
    )
    elastic = jnp.einsum(
        "bshi,bsij->bhj", sources, stiffness.astype(jnp.float32), precision=FULL_PRECISION
    )
    kinetic = jnp.einsum(
        "bhi,bij->bhj", own_blocks, mass_tiles.astype(jnp.float32), precision=FULL_PRECISION
    )
    coupled = elastic - inertia[None, :, None] * kinetic
    residual = field_view(coupled) + forces - own_loads
    stiff_diag = jnp.diagonal(stiffness[:, 0].astype(jnp.float32), axis1=-2, axis2=-1)
    mass_diag = jnp.diagonal(mass_tiles.astype(jnp.float32), axis1=-2, axis2=-1)
    pivots = stiff_diag[:, None, :] - inertia[None, :, None] * mass_diag[:, None, :]
    return (residual, own_field - residual / field_view(pivots))


def per_device(
    initial_guess,
    harmonic_loads,
    stiffness,
    mass_tiles,
    block_links,
    states,
    preload,
    normal_stiff,
    tangent_stiff,
    friction,
):
    coeff_count = initial_guess.shape[0]
    samples_dev = states.shape[0]
    total_samples = samples_dev * lax.axis_size("tm")
    own_field = initial_guess[:, :, 0, :]
    own_loads = harmonic_loads[:, :, 0, :]
    zone_states = states[:, 0, :]
    zone_preload = preload[0]
    zone_normal = normal_stiff[0]
    zone_tangent = tangent_stiff[0]
    zone_friction = friction[0]
    local_stiffness = stiffness[0]
    local_mass = mass_tiles[0]
    local_links = block_links[0]
    synthesis = synthesis_table(
        lax.axis_index("tm") * samples_dev, samples_dev, total_samples, coeff_count
    )
    analysis = analysis_table(synthesis, coeff_count, total_samples)
    residual = own_field
    for iteration in range(ITERS):
        zone_coeffs = lax.all_gather(own_field, "tm", axis=2, tiled=True)
        sectors = padded(own_field[:, :, None, :], (("zone", 2),), 1)
        motion = jnp.einsum("th,hdn->tdn", synthesis, zone_coeffs, precision=FULL_PRECISION)
        forces_time = contact_law(
            motion, zone_states, zone_preload, zone_normal, zone_tangent, zone_friction
        )
        partial_terms = jnp.einsum("th,tdn->hdn", analysis, forces_time, precision=FULL_PRECISION)
        forces = lax.psum_scatter(partial_terms, "tm", scatter_dimension=2, tiled=True)
        residual, own_field = coupled_update(
            own_field,
            zone_coeffs,
            sectors,
            local_stiffness,
            local_mass,
            local_links,
            forces,
            own_loads,
        )
    return (own_field[:, :, None, :], residual[:, :, None, :])


def solution(mesh):
    return jax.shard_map(
        per_device,
        mesh=mesh,
        in_specs=(
            P(None, None, "zone", "tm"),
            P(None, None, "zone", "tm"),
            P("zone", "tm", None, None, None),
            P("zone", "tm", None, None),
            P("zone", "tm", None),
            P("tm", "zone", None),
            P("zone", None),
            P("zone", None),
            P("zone", None),
            P("zone", None),
        ),
        out_specs=(P(None, None, "zone", "tm"), P(None, None, "zone", "tm")),
        check_vma=False,
    )
```

profile of v0, /device:TPU:0, one launch (start us, length us, event | category | flops | bytes accessed | tf_op | source)
XLA Modules:
  0.0 127.1 jit_solution(10812076237233174816)
XLA Ops:
  7.2 0.0 copy-start.5
  7.2 0.0 copy-start.7
  7.2 0.0 copy-start.10
  7.2 0.0 copy-start.12
  7.2 0.0 reduce-scatter.3.cloned.1.call-start
  7.3 3.0 %collective-permute-start = (f32[15,3,1,128]{3,2,1,0:T(1,128)}, f32[15,3,1,128]{3,2,1,0:T(1,128)}, u32[]{:S(2)}, u32[]{:S(2)}) collective-permute-start(f32[15,3,1,128]{3,2,1,0:T(1,128)} %param.10), channel_id=1, source_target_pairs={{0,1},{1,2},{2,3},{3,0},{4,5},{5,6},{6,7},{7,4},{8,9},{9,10},{10,1... | collective-permute-start | bytes 69128 | tf_op jit(solution)/shard_map/ppermute | solution.py:22
  10.3 1.0 collective-permute-start.1
  11.3 0.8 copy.41
  12.1 14.8 %all-gather = f32[15,3,1,1024]{3,0,1,2:T(8,128)S(1)} all-gather(f32[15,3,1,128]{3,0,1,2:T(8,128)S(1)} %copy.41), channel_id=2, replica_groups=mesh['tm'=8,'zone'=4] {'tm'}, dimensions={3}, use_global_device_ids=true | all-gather | bytes 207360 | tf_op jit(solution)/shard_map/all_gather | solution.py:138
  26.9 2.8 %fusion.35 = f32[256,3,1024]{2,0,1:T(8,128)S(1)} fusion(f32[15,3,1,1024]{3,0,1,2:T(8,128)S(1)} %all-gather, s32[15]{0:T(128)S(1)} %and_select_fusion.1, s32[256]{0:T(256)S(1)} %iota_add_fusion, pred[15]{0:T(512)(128)(4,1)S(1)} %compare_and_fusion), kind=kOutput, calls=%fused_computation.45 | convolution fusion | flops 141615360 | bytes 3331147 | tf_op jit(solution)/shard_map/th,hdn->tdn/dot_general | solution.py:140
  29.7 0.8 fusion.31
  30.5 0.5 fusion.30
  31.1 0.0 copy-start.21
  31.1 0.0 copy-start
  31.1 0.0 copy-start.1
  31.1 0.0 copy-done.17
  31.1 0.0 copy-done.19
  31.1 0.0 copy-done.22
  31.1 0.0 copy-done.15
  31.2 0.0 copy-start.3
  31.2 2.4 %fusion = f32[15,3,1024]{2,0,1:T(8,128)} fusion(f32[256,1,1024]{2,0,1:T(8,128)S(1)} %fusion.30, f32[256,1,1024]{2,0,1:T(8,128)S(1)} %get-tuple-element.12, f32[256,1,1024]{2,0,1:T(8,128)S(1)} %get-tuple-element.13, f32[15]{0:T(128)S(1)} %fusion.63, s32[15]{0:T(128)S(1)} %and_select_fusion.1, s32[256]{0:T(256)S(1)} %iota_add_fusion, ...), kind=kOutput, calls=%fused_computation.4 | convolution fusion | flops 143192064 | bytes 3331207 | tf_op jit(solution)/shard_map/th,tdn->hdn/dot_general | solution.py:144
  33.5 0.0 reduce-scatter.3.cloned.1.call-update
  33.6 0.0 reduce-scatter.5.cloned.1.call-start
  33.7 0.6 pad_clamp_fusion
  34.3 0.7 copy_bitcast_fusion.1
  35.1 0.6 multiply_multiply_fusion
  35.6 0.1 reduce
  35.7 1.6 %copy.44 = f32[8,15,384]{2,1,0:T(8,128)} copy(f32[8,15,384]{2,0,1:T(8,128)} %copy_bitcast_fusion.1) | data formatting | bytes 368640 | tf_op jit(solution)/shard_map/reshape | solution.py:69
  37.4 4.6 %gather_fusion.1 = f32[384]{0:T(512)} fusion(f32[384,384]{1,0:T(8,128)S(1)} %fusion.32, s32[384]{0:T(512)S(1)} %or_reduce_fusion), kind=kCustom, calls=%fused_computation.1 | custom fusion | bytes 6144 | tf_op jit(solution)/shard_map/jit(diagonal)/gather | solution.py:101
  42.0 0.0 copy-start.18
  42.0 0.0 copy-start.20
  42.0 3.4 %gather_fusion.2 = f32[384]{0:T(512)S(1)} fusion(f32[384,384]{1,0:T(8,128)S(1)} %bitcast_convert_fusion, s32[384]{0:T(512)S(1)} %or_reduce_fusion), kind=kCustom, calls=%fused_computation.2 | custom fusion | bytes 6144 | tf_op jit(solution)/shard_map/jit(diagonal)/gather | solution.py:102
  45.4 0.0 copy-start.6
  45.5 0.0 copy-start.8
  45.5 0.0 copy-start.11
  45.5 0.0 copy-start.13
  45.5 1.6 %gather_fusion = f32[2,15,384]{2,1,0:T(8,128)S(1)} fusion(f32[8,15,384]{2,1,0:T(8,128)} %copy.44, s32[1024]{0:T(1024)} %pad_clamp_fusion), kind=kCustom, calls=%fused_computation | custom fusion | bytes 92168 | tf_op jit(solution)/shard_map/gather | solution.py:89
  47.1 0.0 collective-permute-done
  47.1 0.7 copy.46
  47.9 0.0 collective-permute-done.1
  47.9 0.7 copy.47
  48.6 0.7 fusion.16
  49.3 0.3 fusion.22
  49.6 14.5 %reduce-scatter.3.cloned.1.call-done = f32[15,3,128]{2,0,1:T(8,128)} async-done(((f32[15,3,1024]{2,0,1:T(8,128)}), f32[15,3,128]{2,0,1:T(8,128)}) %reduce-scatter.3.cloned.1.call-update) | async-done | bytes 23056 | tf_op jit(solution)/shard_map/reduce_scatter | solution.py:145
  64.1 0.8 fusion.50
  64.9 2.4 %collective-permute-start.3 = (f32[15,3,1,128]{3,0,1,2:T(8,128)S(1)}, f32[15,3,1,128]{3,0,1,2:T(8,128)S(1)}, u32[]{:S(2)}, u32[]{:S(2)}) collective-permute-start(f32[15,3,1,128]{3,0,1,2:T(8,128)S(1)} %bitcast.104), channel_id=1, source_target_pairs={{1,0},{2,1},{3,2},{0,3},{5,4},{6,5},{7,6},{4,7},{9,8},{10,9},{11,1... | collective-permute-start | bytes 69128 | tf_op jit(solution)/shard_map/ppermute | solution.py:24
  67.3 0.0 collective-permute-start.2
  67.3 14.3 %all_gather.7 = f32[15,3,1024]{2,0,1:T(8,128)S(1)} all-gather(f32[15,3,128]{2,0,1:T(8,128)S(1)} %fusion.50), channel_id=1, replica_groups=mesh['tm'=8,'zone'=4] {'tm'}, dimensions={2}, use_global_device_ids=true | all-gather | bytes 207360 | tf_op jit(solution)/shard_map/all_gather | solution.py:138
  81.6 0.0 copy-done.18
  81.6 2.8 %fusion.54 = f32[256,3,1024]{2,0,1:T(8,128)S(1)} fusion(f32[15,3,1024]{2,0,1:T(8,128)S(1)} %all_gather.7, s32[15]{0:T(128)S(1)} %copy-done.18, s32[256]{0:T(256)S(1)} %copy-done.16, pred[15]{0:T(512)(128)(4,1)S(1)} %copy-done.20), kind=kOutput, calls=%fused_computation.79 | convolution fusion | flops 141615360 | bytes 3331147 | tf_op jit(solution)/shard_map/th,hdn->tdn/dot_general | solution.py:140
  84.5 0.7 fusion.29
  85.2 0.5 fusion.28
  85.7 0.1 copy-done.23
  85.8 2.4 %fusion.6 = f32[15,3,1024]{2,0,1:T(8,128)} fusion(f32[256,1,1024]{2,0,1:T(8,128)S(1)} %fusion.28, f32[256,1,1024]{2,0,1:T(8,128)S(1)} %get-tuple-element.10, f32[256,1,1024]{2,0,1:T(8,128)S(1)} %get-tuple-element.11, f32[15]{0:T(128)S(1)} %copy-done.23, s32[15]{0:T(128)S(1)} %copy-done.18, s32[256]{0:T(256)S(1)} %copy-done.16, pred[15]{0:T(512)(128)(4,1)S(1)} %copy-done.20), kind=kOutput, calls=%fused_computation.10 | convolution fusion | flops 143192064 | bytes 3331207 | tf_op jit(solution)/shard_map/th,tdn->hdn/dot_general | solution.py:144
  88.3 0.7 gather_fusion.3
  89.0 0.0 reduce-scatter.5.cloned.1.call-update
  89.0 0.0 collective-permute-done.3
  89.1 0.0 collective-permute-done.2
  89.1 0.7 fusion.19
  89.8 0.3 fusion.23
  90.1 28.1 %reduce-scatter.5.cloned.1.call-done = f32[15,3,128]{2,0,1:T(8,128)} async-done(((f32[15,3,1024]{2,0,1:T(8,128)}), f32[15,3,128]{2,0,1:T(8,128)}) %reduce-scatter.5.cloned.1.call-update) | async-done | bytes 23056 | tf_op jit(solution)/shard_map/reduce_scatter | solution.py:145
  118.2 0.8 subtract_bitcast_fusion
  119.0 0.6 copy.61
  119.7 0.6 copy.62
  (53 shorter events, 0.4 us)
Async XLA Ops:
  7.2 22.5 %copy-start.5 = (f32[1,1024]{1,0:T(1,128)S(1)}, f32[1,1024]{1,0:T(1,128)}, u32[]{:S(2)}) copy-start(f32[1,1024]{1,0:T(1,128)} %param.19) | copy-start | bytes 12292
  7.2 22.5 %copy-start.7 = (f32[1,1024]{1,0:T(1,128)S(1)}, f32[1,1024]{1,0:T(1,128)}, u32[]{:S(2)}) copy-start(f32[1,1024]{1,0:T(1,128)} %param.18) | copy-start | bytes 12292
  7.2 22.5 %copy-start.10 = (f32[1,1024]{1,0:T(1,128)S(1)}, f32[1,1024]{1,0:T(1,128)}, u32[]{:S(2)}) copy-start(f32[1,1024]{1,0:T(1,128)} %param.17) | copy-start | bytes 12292
  7.2 22.5 %copy-start.12 = (f32[1,1024]{1,0:T(1,128)S(1)}, f32[1,1024]{1,0:T(1,128)}, u32[]{:S(2)}) copy-start(f32[1,1024]{1,0:T(1,128)} %param.16) | copy-start | bytes 12292
  7.2 22.5 %copy-start.2 = (s32[256,1,1024]{2,1,0:T(1,128)S(1)}, s32[256,1,1024]{2,1,0:T(1,128)}, u32[]{:S(2)}) copy-start(s32[256,1,1024]{2,1,0:T(1,128)} %param.15) | copy-start | bytes 3145732
  7.2 56.8 %reduce-scatter.3.cloned.1.call-start = ((), (), s32[]{:S(2)}) async-start(), calls=%async_computation.2 | async-start | bytes 221184 | tf_op jit(solution)/shard_map/reduce_scatter | solution.py:145
  7.3 39.9 %collective-permute-start = (f32[15,3,1,128]{3,2,1,0:T(1,128)}, f32[15,3,1,128]{3,2,1,0:T(1,128)}, u32[]{:S(2)}, u32[]{:S(2)}) collective-permute-start(f32[15,3,1,128]{3,2,1,0:T(1,128)} %param.10), channel_id=1, source_target_pairs={{0,1},{1,2},{2,3},{3,0},{4,5},{5,6},{6,7},{7,4},{8,9},{9,10},{10,1... | collective-permute-start | bytes 69128 | tf_op jit(solution)/shard_map/ppermute | solution.py:22
  10.3 37.6 %collective-permute-start.1 = (f32[15,3,1,128]{3,2,1,0:T(1,128)}, f32[15,3,1,128]{3,2,1,0:T(1,128)}, u32[]{:S(2)}, u32[]{:S(2)}) collective-permute-start(f32[15,3,1,128]{3,2,1,0:T(1,128)} %param.10), channel_id=1, source_target_pairs={{1,0},{2,1},{3,2},{0,3},{5,4},{6,5},{7,6},{4,7},{9,8},{10,9},{11,1... | collective-permute-start | bytes 69128 | tf_op jit(solution)/shard_map/ppermute | solution.py:24
  11.3 19.8 %copy-start.17 = (s32[15]{0:T(128)}, s32[15]{0:T(128)S(1)}, u32[]{:S(2)}) copy-start(s32[15]{0:T(128)S(1)} %and_select_fusion.1) | copy-start | bytes 184
  11.3 19.8 %copy-start.19 = (pred[15]{0:T(512)(128)(4,1)}, pred[15]{0:T(512)(128)(4,1)S(1)}, u32[]{:S(2)}) copy-start(pred[15]{0:T(512)(128)(4,1)S(1)} %compare_and_fusion) | copy-start | bytes 49
  11.3 19.8 %copy-start.22 = (f32[15]{0:T(128)}, f32[15]{0:T(128)S(1)}, u32[]{:S(2)}) copy-start(f32[15]{0:T(128)S(1)} %fusion.63) | copy-start | bytes 184
  12.1 19.1 %copy-start.15 = (s32[256]{0:T(256)}, s32[256]{0:T(256)S(1)}, u32[]{:S(2)}) copy-start(s32[256]{0:T(256)S(1)} %iota_add_fusion) | copy-start | bytes 3076
  31.1 2.6 %copy-start.21 = (s32[1,1,2]{2,1,0:T(1,128)S(1)}, s32[1,1,2]{2,1,0:T(1,128)}, u32[]{:S(2)}) copy-start(s32[1,1,2]{2,1,0:T(1,128)} %param.14) | copy-start | bytes 28
  31.1 3.9 %copy-start = (bf16[1,1,5,384,384]{4,3,2,1,0:T(8,128)(2,1)S(1)}, bf16[1,1,5,384,384]{4,3,2,1,0:T(8,128)(2,1)}, u32[]{:S(2)}) copy-start(bf16[1,1,5,384,384]{4,3,2,1,0:T(8,128)(2,1)} %param.12) | copy-start | bytes 4423684
  31.1 3.9 %copy-start.1 = (bf16[1,1,384,384]{3,2,1,0:T(8,128)(2,1)S(1)}, bf16[1,1,384,384]{3,2,1,0:T(8,128)(2,1)}, u32[]{:S(2)}) copy-start(bf16[1,1,384,384]{3,2,1,0:T(8,128)(2,1)} %param.13) | copy-start | bytes 884740
  31.2 4.5 %copy-start.3 = (f32[15,3,1,128]{3,2,1,0:T(1,128)S(1)}, f32[15,3,1,128]{3,2,1,0:T(1,128)}, u32[]{:S(2)}) copy-start(f32[15,3,1,128]{3,2,1,0:T(1,128)} %param.10) | copy-start | bytes 69124
  33.6 84.7 %reduce-scatter.5.cloned.1.call-start = ((), (), s32[]{:S(2)}) async-start(), calls=%async_computation.3 | async-start | bytes 221184 | tf_op jit(solution)/shard_map/reduce_scatter | solution.py:145
  42.0 7.3 %copy-start.14 = (f32[15]{0:T(128)S(1)}, f32[15]{0:T(128)}, u32[]{:S(2)}) copy-start(f32[15]{0:T(128)} %multiply_multiply_fusion) | copy-start | bytes 184
  42.0 22.1 %copy-start.4 = (f32[15,3,1,128]{3,2,1,0:T(1,128)S(1)}, f32[15,3,1,128]{3,2,1,0:T(1,128)}, u32[]{:S(2)}) copy-start(f32[15,3,1,128]{3,2,1,0:T(1,128)} %param.11) | copy-start | bytes 69124
  42.0 22.1 %copy-start.9 = (f32[384]{0:T(512)S(1)}, f32[384]{0:T(512)}, u32[]{:S(2)}) copy-start(f32[384]{0:T(512)} %gather_fusion.1) | copy-start | bytes 4612
  42.0 39.7 %copy-start.16 = (s32[256]{0:T(256)S(1)}, s32[256]{0:T(256)}, u32[]{:S(2)}) copy-start(s32[256]{0:T(256)} %copy-done.15) | copy-start | bytes 3076
  42.0 39.7 %copy-start.18 = (s32[15]{0:T(128)S(1)}, s32[15]{0:T(128)}, u32[]{:S(2)}) copy-start(s32[15]{0:T(128)} %copy-done.17) | copy-start | bytes 184
  42.0 39.7 %copy-start.20 = (pred[15]{0:T(512)(128)(4,1)S(1)}, pred[15]{0:T(512)(128)(4,1)}, u32[]{:S(2)}) copy-start(pred[15]{0:T(512)(128)(4,1)} %copy-done.19) | copy-start | bytes 49
  45.4 39.0 %copy-start.6 = (f32[1,1024]{1,0:T(1,128)S(1)}, f32[1,1024]{1,0:T(1,128)}, u32[]{:S(2)}) copy-start(f32[1,1024]{1,0:T(1,128)} %param.19) | copy-start | bytes 12292
  45.5 39.0 %copy-start.8 = (f32[1,1024]{1,0:T(1,128)S(1)}, f32[1,1024]{1,0:T(1,128)}, u32[]{:S(2)}) copy-start(f32[1,1024]{1,0:T(1,128)} %param.18) | copy-start | bytes 12292
  45.5 39.0 %copy-start.11 = (f32[1,1024]{1,0:T(1,128)S(1)}, f32[1,1024]{1,0:T(1,128)}, u32[]{:S(2)}) copy-start(f32[1,1024]{1,0:T(1,128)} %param.17) | copy-start | bytes 12292
  45.5 39.0 %copy-start.13 = (f32[1,1024]{1,0:T(1,128)S(1)}, f32[1,1024]{1,0:T(1,128)}, u32[]{:S(2)}) copy-start(f32[1,1024]{1,0:T(1,128)} %param.16) | copy-start | bytes 12292
  64.9 24.1 %collective-permute-start.3 = (f32[15,3,1,128]{3,0,1,2:T(8,128)S(1)}, f32[15,3,1,128]{3,0,1,2:T(8,128)S(1)}, u32[]{:S(2)}, u32[]{:S(2)}) collective-permute-start(f32[15,3,1,128]{3,0,1,2:T(8,128)S(1)} %bitcast.104), channel_id=1, source_target_pairs={{1,0},{2,1},{3,2},{0,3},{5,4},{6,5},{7,6},{4,7},{9,8},{10,9},{11,1... | collective-permute-start | bytes 69128 | tf_op jit(solution)/shard_map/ppermute | solution.py:24
  67.3 21.7 %collective-permute-start.2 = (f32[15,3,1,128]{3,0,1,2:T(8,128)S(1)}, f32[15,3,1,128]{3,0,1,2:T(8,128)S(1)}, u32[]{:S(2)}, u32[]{:S(2)}) collective-permute-start(f32[15,3,1,128]{3,0,1,2:T(8,128)S(1)} %bitcast.105), channel_id=1, source_target_pairs={{0,1},{1,2},{2,3},{3,0},{4,5},{5,6},{6,7},{7,4},{8,9},{9,10},{10,1... | collective-permute-start | bytes 69128 | tf_op jit(solution)/shard_map/ppermute | solution.py:22
  85.2 0.6 copy-start.23
Sparse Core Ops, SparseCore 0:
  33.7 30.3 reduce-scatter.2
  89.1 29.0 reduce-scatter.4
where the time goes:
time: 128 us; the launch traced here: 127 us
  waiting for transfers between devices  42.6 us (33%)
  blocking collectives  29.1 us (23%)
  local copies, waits for them, and re-layouts  16.6 us (13%)
  between operations  14.6 us (11%)
  matrix products  12.2 us (10%)
  starting transfers between devices  6.54 us (5%)
  other arithmetic  5.5 us (4%)
    reduce_scatter x2, waiting for transfers between devices, per_device(): lax.psum_scatter(partial_terms, 'tm', scatter_dimension=2, tiled=True)  42.6 us
    all_gather x2, blocking collectives, per_device(): zone_coeffs = lax.all_gather(own_field, 'tm', axis=2, tiled=True)  29.1 us
    dot_general x2, matrix products, per_device(): jnp.einsum('th,hdn->tdn', synthesis, zone_coeffs, precision=FULL_PRECISION)  5.57 us
    dot_general x2, matrix products, per_device(): jnp.einsum('th,tdn->hdn', analysis, forces_time, precision=FULL_PRECISION)  4.74 us
    gather x1, local copies, waits for them, and re-layouts, coupled_update(): jnp.diagonal(stiffness[:, 0].astype(jnp.float32), axis1=-2, axis2=-1)  4.56 us
    ppermute x2, starting transfers between devices, padded(): lax.ppermute(head, axis, [((i + 1) % count, i) for i in range(count)])  3.47 us
    gather x1, local copies, waits for them, and re-layouts, coupled_update(): mass_diag = jnp.diagonal(mass_tiles.astype(jnp.float32), axis1=-2, axis2=-1)  3.45 us
    ppermute x2, starting transfers between devices, padded(): lax.ppermute(tail, axis, [(i, (i + 1) % count) for i in range(count)])  2.99 us
  transfers between devices with their start and end apart: 6, of which 2 were waited for; matrix products, arithmetic and copies ran while one was open for 25% of the time, Pallas kernels for 0%

commit v1 on v0

--- a/solution.py
+++ b/solution.py
@@ -135,7 +135,14 @@
     analysis = analysis_table(synthesis, coeff_count, total_samples)
     residual = own_field
     for iteration in range(ITERS):
-        zone_coeffs = lax.all_gather(own_field, "tm", axis=2, tiled=True)
+        ring = [own_field]
+        for hop in range(7):
+            ring.append(lax.ppermute(ring[-1], "tm", [(dev, (dev + 1) % 8) for dev in range(8)]))
+        zone_coeffs = jnp.roll(
+            jnp.concatenate(ring[::-1], axis=2),
+            (lax.axis_index("tm") + 1) * ring[0].shape[2],
+            axis=2,
+        )
         sectors = padded(own_field[:, :, None, :], (("zone", 2),), 1)
         motion = jnp.einsum("th,hdn->tdn", synthesis, zone_coeffs, precision=FULL_PRECISION)
         forces_time = contact_law(

time: 128 us -> 176 us (1.38)
  waiting for transfers between devices: 42.6 us -> 117 us
  blocking collectives: 29.1 us -> 0 us
  other arithmetic: 5.5 us -> 8.7 us
    ppermute x0 -> x14, waiting for transfers between devices: none -> 57.8 us  [per_device(): lax.ppermute(ring[-1], 'tm', [(dev, (dev + 1) % 8) for dev in range(8)])]
    all_gather x2 -> x0, blocking collectives: 29.1 us -> none  [per_device(): zone_coeffs = lax.all_gather(own_field, 'tm', axis=2, tiled=True)]
    reduce_scatter x2, waiting for transfers between devices: 42.6 us -> 57 us  [per_device(): lax.psum_scatter(partial_terms, 'tm', scatter_dimension=2, tiled=True)]
    ppermute x2, waiting for transfers between devices: 0.01 us -> 1.94 us  [padded(): lax.ppermute(tail, axis, [(i, (i + 1) % count) for i in range(count)])]
  transfers between devices with their start and end apart: 6 -> 20, of which waited for: 2 -> 16; matrix products, arithmetic and copies ran while one was open for 25% -> 9% of each run, Pallas kernels for 0% -> 0%
where the time goes in v1:
time: 176 us; the launch traced here: 175 us
  waiting for transfers between devices  117 us (66%)
  local copies, waits for them, and re-layouts  15.2 us (9%)
  between operations  14.9 us (8%)
  matrix products  13.2 us (8%)
  other arithmetic  8.7 us (5%)
  starting transfers between devices  6.57 us (4%)
    ppermute x14, waiting for transfers between devices, per_device(): lax.ppermute(ring[-1], 'tm', [(dev, (dev + 1) % 8) for dev in range(8)])  57.8 us
    reduce_scatter x2, waiting for transfers between devices, per_device(): lax.psum_scatter(partial_terms, 'tm', scatter_dimension=2, tiled=True)  57 us
    dot_general x2, matrix products, per_device(): jnp.einsum('th,hdn->tdn', synthesis, zone_coeffs, precision=FULL_PRECISION)  6.56 us
    dot_general x2, matrix products, per_device(): jnp.einsum('th,tdn->hdn', analysis, forces_time, precision=FULL_PRECISION)  4.76 us
  transfers between devices with their start and end apart: 20, of which 16 were waited for; matrix products, arithmetic and copies ran while one was open for 9% of the time, Pallas kernels for 0%

profile of v1, /device:TPU:0, one launch (start us, length us, event | category | flops | bytes accessed | tf_op | source)
XLA Modules:
  0.0 175.3 jit_solution(4315655476989934521)
XLA Ops:
  7.2 0.0 reduce-scatter.3.cloned.1.call-start
  7.2 3.0 %collective-permute-start = (f32[15,3,1,128]{3,2,1,0:T(1,128)}, f32[15,3,1,128]{3,2,1,0:T(1,128)S(1)}, u32[]{:S(2)}, u32[]{:S(2)}) collective-permute-start(f32[15,3,1,128]{3,2,1,0:T(1,128)} %param.12), channel_id=1, source_target_pairs={{0,1},{1,2},{2,3},{3,0},{4,5},{5,6},{6,7},{7,4},{8,9},{9,10},{10,1... | collective-permute-start | bytes 69128 | tf_op jit(solution)/shard_map/ppermute | solution.py:22
  10.2 1.0 collective-permute-start.1
  11.2 0.8 copy.81
  12.0 1.0 fusion.32
  13.0 0.0 copy-start.9
  13.0 1.0 bitcast_convert_fusion
  14.0 0.7 fusion.69
  14.7 2.4 %collective-permute-done.2 = f32[15,3,128]{2,0,1:T(8,128)S(1)} collective-permute-done((f32[15,3,128]{2,0,1:T(8,128)S(1)}, f32[15,3,128]{2,0,1:T(8,128)S(1)}, u32[]{:S(2)}, u32[]{:S(2)}) %collective-permute-start.2) | collective-permute-done | bytes 23072 | tf_op jit(solution)/shard_map/ppermute | solution.py:140
  17.1 0.0 copy-start.25
  17.1 5.0 %collective-permute-done.3 = f32[15,3,128]{2,0,1:T(8,128)S(1)} collective-permute-done((f32[15,3,128]{2,0,1:T(8,128)S(1)}, f32[15,3,128]{2,0,1:T(8,128)S(1)}, u32[]{:S(2)}, u32[]{:S(2)}) %collective-permute-start.3) | collective-permute-done | bytes 23072 | tf_op jit(solution)/shard_map/ppermute | solution.py:140
  22.1 5.0 %collective-permute-done.4 = f32[15,3,128]{2,0,1:T(8,128)S(1)} collective-permute-done((f32[15,3,128]{2,0,1:T(8,128)S(1)}, f32[15,3,128]{2,0,1:T(8,128)S(1)}, u32[]{:S(2)}, u32[]{:S(2)}) %collective-permute-start.4) | collective-permute-done | bytes 23072 | tf_op jit(solution)/shard_map/ppermute | solution.py:140
  27.2 5.0 %collective-permute-done.5 = f32[15,3,128]{2,0,1:T(8,128)S(1)} collective-permute-done((f32[15,3,128]{2,0,1:T(8,128)S(1)}, f32[15,3,128]{2,0,1:T(8,128)S(1)}, u32[]{:S(2)}, u32[]{:S(2)}) %collective-permute-start.5) | collective-permute-done | bytes 23072 | tf_op jit(solution)/shard_map/ppermute | solution.py:140
  32.2 5.0 %collective-permute-done.6 = f32[15,3,128]{2,0,1:T(8,128)S(1)} collective-permute-done((f32[15,3,128]{2,0,1:T(8,128)S(1)}, f32[15,3,128]{2,0,1:T(8,128)S(1)}, u32[]{:S(2)}, u32[]{:S(2)}) %collective-permute-start.6) | collective-permute-done | bytes 23072 | tf_op jit(solution)/shard_map/ppermute | solution.py:140
  37.3 5.0 %collective-permute-done.7 = f32[15,3,128]{2,0,1:T(8,128)S(1)} collective-permute-done((f32[15,3,128]{2,0,1:T(8,128)S(1)}, f32[15,3,128]{2,0,1:T(8,128)S(1)}, u32[]{:S(2)}, u32[]{:S(2)}) %collective-permute-start.7) | collective-permute-done | bytes 23072 | tf_op jit(solution)/shard_map/ppermute | solution.py:140
  42.3 0.7 copy.40
  43.1 0.8 reduce
  43.9 3.4 %gather_fusion.1 = f32[384]{0:T(512)S(1)} fusion(f32[384,384]{1,0:T(8,128)S(1)} %fusion.32, s32[384]{0:T(512)S(1)} %or_reduce_fusion), kind=kCustom, calls=%fused_computation.1 | custom fusion | bytes 6144 | tf_op jit(solution)/shard_map/jit(diagonal)/gather | solution.py:101
  47.4 3.4 %gather_fusion.2 = f32[384]{0:T(512)S(1)} fusion(f32[384,384]{1,0:T(8,128)S(1)} %bitcast_convert_fusion, s32[384]{0:T(512)S(1)} %or_reduce_fusion), kind=kCustom, calls=%fused_computation.2 | custom fusion | bytes 6144 | tf_op jit(solution)/shard_map/jit(diagonal)/gather | solution.py:102
  50.9 0.0 copy-start.13
  50.9 0.0 copy-start.15
  51.1 0.1 fusion.36
  51.3 2.8 %fusion.56 = f32[256,3,1024]{2,0,1:T(8,128)S(1)} fusion(f32[15,3,1024]{2,0,1:T(8,128)S(1)} %fusion.36, s32[15]{0:T(128)S(1)} %and_select_fusion.1, s32[256]{0:T(256)S(1)} %iota_add_fusion, pred[15]{0:T(512)(128)(4,1)S(1)} %compare_and_fusion), kind=kOutput, calls=%fused_computation.102 | convolution fusion | flops 141615360 | bytes 3331147 | tf_op jit(solution)/shard_map/th,hdn->tdn/dot_general | solution.py:147
  54.1 0.8 fusion.31
  54.9 0.5 fusion.30
  55.4 0.2 copy-done.2
  55.7 2.4 %fusion = f32[15,3,1024]{2,0,1:T(8,128)} fusion(f32[256,1,1024]{2,0,1:T(8,128)S(1)} %fusion.30, f32[256,1,1024]{2,0,1:T(8,128)S(1)} %get-tuple-element.13, f32[256,1,1024]{2,0,1:T(8,128)S(1)} %get-tuple-element.14, f32[15]{0:T(128)S(1)} %fusion.68, s32[15]{0:T(128)S(1)} %and_select_fusion.1, s32[256]{0:T(256)S(1)} %iota_add_fusion, ...), kind=kOutput, calls=%fused_computation.4 | convolution fusion | flops 143192064 | bytes 3331207 | tf_op jit(solution)/shard_map/th,tdn->hdn/dot_general | solution.py:151
  58.0 0.0 reduce-scatter.3.cloned.1.call-update
  58.1 0.0 reduce-scatter.5.cloned.1.call-start
  58.1 0.6 gather_fusion
  58.7 0.7 fusion.16
  59.4 0.2 fusion.22
  59.7 29.5 %reduce-scatter.3.cloned.1.call-done = f32[15,3,128]{2,0,1:T(8,128)} async-done(((f32[15,3,1024]{2,0,1:T(8,128)}), f32[15,3,128]{2,0,1:T(8,128)}) %reduce-scatter.3.cloned.1.call-update) | async-done | bytes 23056 | tf_op jit(solution)/shard_map/reduce_scatter | solution.py:152
  89.2 0.8 fusion.50
  90.0 0.1 collective-permute-start.11
  90.1 5.0 %collective-permute-done.11 = f32[15,3,128]{2,0,1:T(8,128)S(1)} collective-permute-done((f32[15,3,128]{2,0,1:T(8,128)S(1)}, f32[15,3,128]{2,0,1:T(8,128)S(1)}, u32[]{:S(2)}, u32[]{:S(2)}) %collective-permute-start.11) | collective-permute-done | bytes 23072 | tf_op jit(solution)/shard_map/ppermute | solution.py:140
  95.1 5.0 %collective-permute-done.12 = f32[15,3,128]{2,0,1:T(8,128)S(1)} collective-permute-done((f32[15,3,128]{2,0,1:T(8,128)S(1)}, f32[15,3,128]{2,0,1:T(8,128)S(1)}, u32[]{:S(2)}, u32[]{:S(2)}) %collective-permute-start.12) | collective-permute-done | bytes 23072 | tf_op jit(solution)/shard_map/ppermute | solution.py:140
  100.2 5.0 %collective-permute-done.13 = f32[15,3,128]{2,0,1:T(8,128)S(1)} collective-permute-done((f32[15,3,128]{2,0,1:T(8,128)S(1)}, f32[15,3,128]{2,0,1:T(8,128)S(1)}, u32[]{:S(2)}, u32[]{:S(2)}) %collective-permute-start.13) | collective-permute-done | bytes 23072 | tf_op jit(solution)/shard_map/ppermute | solution.py:140
  105.2 5.0 %collective-permute-done.14 = f32[15,3,128]{2,0,1:T(8,128)S(1)} collective-permute-done((f32[15,3,128]{2,0,1:T(8,128)S(1)}, f32[15,3,128]{2,0,1:T(8,128)S(1)}, u32[]{:S(2)}, u32[]{:S(2)}) %collective-permute-start.14) | collective-permute-done | bytes 23072 | tf_op jit(solution)/shard_map/ppermute | solution.py:140
  110.3 5.0 %collective-permute-done.15 = f32[15,3,128]{2,0,1:T(8,128)S(1)} collective-permute-done((f32[15,3,128]{2,0,1:T(8,128)S(1)}, f32[15,3,128]{2,0,1:T(8,128)S(1)}, u32[]{:S(2)}, u32[]{:S(2)}) %collective-permute-start.15) | collective-permute-done | bytes 23072 | tf_op jit(solution)/shard_map/ppermute | solution.py:140
  115.3 2.4 %collective-permute-start.10 = (f32[15,3,1,128]{3,0,1,2:T(8,128)S(1)}, f32[15,3,1,128]{3,0,1,2:T(8,128)S(1)}, u32[]{:S(2)}, u32[]{:S(2)}) collective-permute-start(f32[15,3,1,128]{3,0,1,2:T(8,128)S(1)} %bitcast.107), channel_id=1, source_target_pairs={{1,0},{2,1},{3,2},{0,3},{5,4},{6,5},{7,6},{4,7},{9,8},{10,9},{11,1... | collective-permute-start | bytes 69128 | tf_op jit(solution)/shard_map/ppermute | solution.py:24
  117.7 2.7 %collective-permute-done.16 = f32[15,3,128]{2,0,1:T(8,128)S(1)} collective-permute-done((f32[15,3,128]{2,0,1:T(8,128)S(1)}, f32[15,3,128]{2,0,1:T(8,128)S(1)}, u32[]{:S(2)}, u32[]{:S(2)}) %collective-permute-start.16) | collective-permute-done | bytes 23072 | tf_op jit(solution)/shard_map/ppermute | solution.py:140
  120.5 1.9 %collective-permute-done.9 = f32[15,3,1,128]{3,0,1,2:T(8,128)S(1)} collective-permute-done((f32[15,3,1,128]{3,0,1,2:T(8,128)S(1)}, f32[15,3,1,128]{3,0,1,2:T(8,128)S(1)}, u32[]{:S(2)}, u32[]{:S(2)}) %collective-permute-start.9) | collective-permute-done | bytes 23072 | tf_op jit(solution)/shard_map/ppermute | solution.py:22
  122.4 0.6 broadcast_in_dim_reshape_transpose_reshape_squeeze.20
  123.1 2.4 %collective-permute-done.17 = f32[15,3,128]{2,0,1:T(8,128)S(1)} collective-permute-done((f32[15,3,128]{2,0,1:T(8,128)S(1)}, f32[15,3,128]{2,0,1:T(8,128)S(1)}, u32[]{:S(2)}, u32[]{:S(2)}) %collective-permute-start.17) | collective-permute-done | bytes 23072 | tf_op jit(solution)/shard_map/ppermute | solution.py:140
  125.5 0.1 fusion.35
  125.6 0.7 copy-done.6
  126.2 0.7 reshape.346
  127.0 3.8 %fusion.54 = f32[256,3,1024]{2,0,1:T(8,128)S(1)} fusion(f32[15,3,1024]{2,0,1:T(8,128)} %copy-done.6, s32[15]{0:T(128)} %copy-done.28, s32[256]{0:T(256)} %copy-done.26, pred[15]{0:T(512)(128)(4,1)} %copy-done.30), kind=kOutput, calls=%fused_computation.100 | convolution fusion | flops 141615360 | bytes 3331147 | tf_op jit(solution)/shard_map/th,hdn->tdn/dot_general | solution.py:147
  130.8 0.7 copy.51
  131.5 1.6 gather_fusion.3
  133.1 1.6 fusion.29
  134.8 0.5 fusion.28
  135.3 0.0 copy-start.1
  135.4 0.0 copy-done.27
  135.4 0.0 copy-done.33
  135.4 2.4 %fusion.6 = f32[15,3,1024]{2,0,1:T(8,128)} fusion(f32[256,1,1024]{2,0,1:T(8,128)S(1)} %fusion.28, f32[256,1,1024]{2,0,1:T(8,128)S(1)} %get-tuple-element.11, f32[256,1,1024]{2,0,1:T(8,128)S(1)} %get-tuple-element.12, f32[15]{0:T(128)S(1)} %copy-done.33, s32[15]{0:T(128)S(1)} %copy-done.29, s32[256]{0:T(256)S(1)} %copy-done.27, pred[15]{0:T(512)(128)(4,1)S(1)} %copy-done.31), kind=kOutput, calls=%fused_computation.10 | convolution fusion | flops 143192064 | bytes 3331207 | tf_op jit(solution)/shard_map/th,tdn->hdn/dot_general | solution.py:151
  137.8 0.0 reduce-scatter.5.cloned.1.call-update
  137.9 0.7 fusion.19
  138.6 0.2 fusion.23
  138.8 27.5 %reduce-scatter.5.cloned.1.call-done = f32[15,3,128]{2,0,1:T(8,128)} async-done(((f32[15,3,1024]{2,0,1:T(8,128)}), f32[15,3,128]{2,0,1:T(8,128)}) %reduce-scatter.5.cloned.1.call-update) | async-done | bytes 23056 | tf_op jit(solution)/shard_map/reduce_scatter | solution.py:152
  166.4 0.8 subtract_bitcast_fusion
  167.2 0.6 copy.56
  167.8 0.6 copy.57
  (117 shorter events, 0.6 us)
Async XLA Ops:
  7.2 82.0 %reduce-scatter.3.cloned.1.call-start = ((), (), s32[]{:S(2)}) async-start(), calls=%async_computation.2 | async-start | bytes 221184 | tf_op jit(solution)/shard_map/reduce_scatter | solution.py:152
  7.2 43.7 %collective-permute-start = (f32[15,3,1,128]{3,2,1,0:T(1,128)}, f32[15,3,1,128]{3,2,1,0:T(1,128)S(1)}, u32[]{:S(2)}, u32[]{:S(2)}) collective-permute-start(f32[15,3,1,128]{3,2,1,0:T(1,128)} %param.12), channel_id=1, source_target_pairs={{0,1},{1,2},{2,3},{3,0},{4,5},{5,6},{6,7},{7,4},{8,9},{9,10},{10,1... | collective-permute-start | bytes 69128 | tf_op jit(solution)/shard_map/ppermute | solution.py:22
  10.2 40.8 %collective-permute-start.1 = (f32[15,3,1,128]{3,2,1,0:T(1,128)}, f32[15,3,1,128]{3,2,1,0:T(1,128)S(1)}, u32[]{:S(2)}, u32[]{:S(2)}) collective-permute-start(f32[15,3,1,128]{3,2,1,0:T(1,128)} %param.12), channel_id=1, source_target_pairs={{1,0},{2,1},{3,2},{0,3},{5,4},{6,5},{7,6},{4,7},{9,8},{10,9},{11,1... | collective-permute-start | bytes 69128 | tf_op jit(solution)/shard_map/ppermute | solution.py:24
  12.0 5.0 %collective-permute-start.2 = (f32[15,3,128]{2,0,1:T(8,128)S(1)}, f32[15,3,128]{2,0,1:T(8,128)S(1)}, u32[]{:S(2)}, u32[]{:S(2)}) collective-permute-start(f32[15,3,128]{2,0,1:T(8,128)S(1)} %bitcast.124), channel_id=1, source_target_pairs={{0,4},{4,8},{8,12},{12,16},{16,20},{20,24},{24,28},{28,0},{1,5},{5... | collective-permute-start | bytes 69128 | tf_op jit(solution)/shard_map/ppermute | solution.py:140
  13.0 38.1 %copy-start.9 = (f32[15,3,1,128]{3,2,1,0:T(1,128)S(1)}, f32[15,3,1,128]{3,2,1,0:T(1,128)}, u32[]{:S(2)}) copy-start(f32[15,3,1,128]{3,2,1,0:T(1,128)} %param.12) | copy-start | bytes 69124
  17.0 5.0 %collective-permute-start.3 = (f32[15,3,128]{2,0,1:T(8,128)S(1)}, f32[15,3,128]{2,0,1:T(8,128)S(1)}, u32[]{:S(2)}, u32[]{:S(2)}) collective-permute-start(f32[15,3,128]{2,0,1:T(8,128)S(1)} %collective-permute-done.2), channel_id=1, source_target_pairs={{0,4},{4,8},{8,12},{12,16},{16,20},{20,24},{24,28},{28,0},{1,5},{5... | collective-permute-start | bytes 69128 | tf_op jit(solution)/shard_map/ppermute | solution.py:140
  17.1 41.1 %copy-start.25 = (s32[1024]{0:T(1024)}, s32[1024]{0:T(1024)S(1)}, u32[]{:S(2)}) copy-start(s32[1024]{0:T(1024)S(1)} %pad_clamp_fusion) | copy-start | bytes 12292
  22.1 5.0 %collective-permute-start.4 = (f32[15,3,128]{2,0,1:T(8,128)S(1)}, f32[15,3,128]{2,0,1:T(8,128)S(1)}, u32[]{:S(2)}, u32[]{:S(2)}) collective-permute-start(f32[15,3,128]{2,0,1:T(8,128)S(1)} %collective-permute-done.3), channel_id=1, source_target_pairs={{0,4},{4,8},{8,12},{12,16},{16,20},{20,24},{24,28},{28,0},{1,5},{5... | collective-permute-start | bytes 69128 | tf_op jit(solution)/shard_map/ppermute | solution.py:140
  22.1 33.5 %copy-start.26 = (s32[256]{0:T(256)}, s32[256]{0:T(256)S(1)}, u32[]{:S(2)}) copy-start(s32[256]{0:T(256)S(1)} %iota_add_fusion) | copy-start | bytes 3076
  27.1 5.0 %collective-permute-start.5 = (f32[15,3,128]{2,0,1:T(8,128)S(1)}, f32[15,3,128]{2,0,1:T(8,128)S(1)}, u32[]{:S(2)}, u32[]{:S(2)}) collective-permute-start(f32[15,3,128]{2,0,1:T(8,128)S(1)} %collective-permute-done.4), channel_id=1, source_target_pairs={{0,4},{4,8},{8,12},{12,16},{16,20},{20,24},{24,28},{28,0},{1,5},{5... | collective-permute-start | bytes 69128 | tf_op jit(solution)/shard_map/ppermute | solution.py:140
  27.2 62.0 %copy-start.23 = (f32[15]{0:T(128)}, f32[15]{0:T(128)S(1)}, u32[]{:S(2)}) copy-start(f32[15]{0:T(128)S(1)} %multiply_multiply_fusion) | copy-start | bytes 184
  32.2 5.0 %collective-permute-start.6 = (f32[15,3,128]{2,0,1:T(8,128)S(1)}, f32[15,3,128]{2,0,1:T(8,128)S(1)}, u32[]{:S(2)}, u32[]{:S(2)}) collective-permute-start(f32[15,3,128]{2,0,1:T(8,128)S(1)} %collective-permute-done.5), channel_id=1, source_target_pairs={{0,4},{4,8},{8,12},{12,16},{16,20},{20,24},{24,28},{28,0},{1,5},{5... | collective-permute-start | bytes 69128 | tf_op jit(solution)/shard_map/ppermute | solution.py:140
  32.2 23.4 %copy-start.28 = (s32[15]{0:T(128)}, s32[15]{0:T(128)S(1)}, u32[]{:S(2)}) copy-start(s32[15]{0:T(128)S(1)} %and_select_fusion.1) | copy-start | bytes 184
  37.2 5.0 %collective-permute-start.7 = (f32[15,3,128]{2,0,1:T(8,128)S(1)}, f32[15,3,128]{2,0,1:T(8,128)S(1)}, u32[]{:S(2)}, u32[]{:S(2)}) collective-permute-start(f32[15,3,128]{2,0,1:T(8,128)S(1)} %collective-permute-done.6), channel_id=1, source_target_pairs={{0,4},{4,8},{8,12},{12,16},{16,20},{20,24},{24,28},{28,0},{1,5},{5... | collective-permute-start | bytes 69128 | tf_op jit(solution)/shard_map/ppermute | solution.py:140
  37.3 18.4 %copy-start.30 = (pred[15]{0:T(512)(128)(4,1)}, pred[15]{0:T(512)(128)(4,1)S(1)}, u32[]{:S(2)}) copy-start(pred[15]{0:T(512)(128)(4,1)S(1)} %compare_and_fusion) | copy-start | bytes 49
  42.3 8.7 %collective-permute-start.8 = (f32[15,3,128]{2,0,1:T(8,128)S(1)}, f32[15,3,128]{2,0,1:T(8,128)S(1)}, u32[]{:S(2)}, u32[]{:S(2)}) collective-permute-start(f32[15,3,128]{2,0,1:T(8,128)S(1)} %collective-permute-done.7), channel_id=1, source_target_pairs={{0,4},{4,8},{8,12},{12,16},{16,20},{20,24},{24,28},{28,0},{1,5},{5... | collective-permute-start | bytes 69128 | tf_op jit(solution)/shard_map/ppermute | solution.py:140
  42.3 13.3 %copy-start.32 = (f32[15]{0:T(128)}, f32[15]{0:T(128)S(1)}, u32[]{:S(2)}) copy-start(f32[15]{0:T(128)S(1)} %fusion.68) | copy-start | bytes 184
  47.4 41.8 %copy-start.17 = (f32[384]{0:T(512)}, f32[384]{0:T(512)S(1)}, u32[]{:S(2)}) copy-start(f32[384]{0:T(512)S(1)} %gather_fusion.1) | copy-start | bytes 4612
  50.8 38.3 %copy-start.19 = (f32[384]{0:T(512)}, f32[384]{0:T(512)S(1)}, u32[]{:S(2)}) copy-start(f32[384]{0:T(512)S(1)} %gather_fusion.2) | copy-start | bytes 4612
  50.9 3.2 %copy-start.7 = (s32[256,1,1024]{2,1,0:T(1,128)S(1)}, s32[256,1,1024]{2,1,0:T(1,128)}, u32[]{:S(2)}) copy-start(s32[256,1,1024]{2,1,0:T(1,128)} %param.17) | copy-start | bytes 3145732
  50.9 3.2 %copy-start.13 = (f32[1,1024]{1,0:T(1,128)S(1)}, f32[1,1024]{1,0:T(1,128)}, u32[]{:S(2)}) copy-start(f32[1,1024]{1,0:T(1,128)} %param.21) | copy-start | bytes 12292
  50.9 3.2 %copy-start.15 = (f32[1,1024]{1,0:T(1,128)S(1)}, f32[1,1024]{1,0:T(1,128)}, u32[]{:S(2)}) copy-start(f32[1,1024]{1,0:T(1,128)} %param.20) | copy-start | bytes 12292
  50.9 3.2 %copy-start.21 = (f32[1,1024]{1,0:T(1,128)S(1)}, f32[1,1024]{1,0:T(1,128)}, u32[]{:S(2)}) copy-start(f32[1,1024]{1,0:T(1,128)} %param.19) | copy-start | bytes 12292
  50.9 3.2 %copy-start.22 = (f32[1,1024]{1,0:T(1,128)S(1)}, f32[1,1024]{1,0:T(1,128)}, u32[]{:S(2)}) copy-start(f32[1,1024]{1,0:T(1,128)} %param.18) | copy-start | bytes 12292
  54.9 0.7 copy-start.2
  55.6 3.1 %copy-start = (bf16[1,1,5,384,384]{4,3,2,1,0:T(8,128)(2,1)S(1)}, bf16[1,1,5,384,384]{4,3,2,1,0:T(8,128)(2,1)}, u32[]{:S(2)}) copy-start(bf16[1,1,5,384,384]{4,3,2,1,0:T(8,128)(2,1)} %param.14) | copy-start | bytes 4423684
  55.6 3.8 %copy-start.4 = (bf16[1,1,384,384]{3,2,1,0:T(8,128)(2,1)S(1)}, bf16[1,1,384,384]{3,2,1,0:T(8,128)(2,1)}, u32[]{:S(2)}) copy-start(bf16[1,1,384,384]{3,2,1,0:T(8,128)(2,1)} %param.15) | copy-start | bytes 884740
  55.6 33.6 %copy-start.11 = (f32[15,3,1,128]{3,2,1,0:T(1,128)S(1)}, f32[15,3,1,128]{3,2,1,0:T(1,128)}, u32[]{:S(2)}) copy-start(f32[15,3,1,128]{3,2,1,0:T(1,128)} %param.13) | copy-start | bytes 69124
  58.1 108.3 %reduce-scatter.5.cloned.1.call-start = ((), (), s32[]{:S(2)}) async-start(), calls=%async_computation.3 | async-start | bytes 221184 | tf_op jit(solution)/shard_map/reduce_scatter | solution.py:152
  90.0 5.1 %collective-permute-start.11 = (f32[15,3,128]{2,0,1:T(8,128)S(1)}, f32[15,3,128]{2,0,1:T(8,128)S(1)}, u32[]{:S(2)}, u32[]{:S(2)}) collective-permute-start(f32[15,3,128]{2,0,1:T(8,128)S(1)} %fusion.50), channel_id=1, source_target_pairs={{0,4},{4,8},{8,12},{12,16},{16,20},{20,24},{24,28},{28,0},{1,5},{5... | collective-permute-start | bytes 69128 | tf_op jit(solution)/shard_map/ppermute | solution.py:140
  95.1 5.0 %collective-permute-start.12 = (f32[15,3,128]{2,0,1:T(8,128)S(1)}, f32[15,3,128]{2,0,1:T(8,128)S(1)}, u32[]{:S(2)}, u32[]{:S(2)}) collective-permute-start(f32[15,3,128]{2,0,1:T(8,128)S(1)} %collective-permute-done.11), channel_id=1, source_target_pairs={{0,4},{4,8},{8,12},{12,16},{16,20},{20,24},{24,28},{28,0},{1,5},{5... | collective-permute-start | bytes 69128 | tf_op jit(solution)/shard_map/ppermute | solution.py:140
  100.2 5.0 %collective-permute-start.13 = (f32[15,3,128]{2,0,1:T(8,128)S(1)}, f32[15,3,128]{2,0,1:T(8,128)S(1)}, u32[]{:S(2)}, u32[]{:S(2)}) collective-permute-start(f32[15,3,128]{2,0,1:T(8,128)S(1)} %collective-permute-done.12), channel_id=1, source_target_pairs={{0,4},{4,8},{8,12},{12,16},{16,20},{20,24},{24,28},{28,0},{1,5},{5... | collective-permute-start | bytes 69128 | tf_op jit(solution)/shard_map/ppermute | solution.py:140
  105.2 5.0 %collective-permute-start.14 = (f32[15,3,128]{2,0,1:T(8,128)S(1)}, f32[15,3,128]{2,0,1:T(8,128)S(1)}, u32[]{:S(2)}, u32[]{:S(2)}) collective-permute-start(f32[15,3,128]{2,0,1:T(8,128)S(1)} %collective-permute-done.13), channel_id=1, source_target_pairs={{0,4},{4,8},{8,12},{12,16},{16,20},{20,24},{24,28},{28,0},{1,5},{5... | collective-permute-start | bytes 69128 | tf_op jit(solution)/shard_map/ppermute | solution.py:140
  110.3 5.0 %collective-permute-start.15 = (f32[15,3,128]{2,0,1:T(8,128)S(1)}, f32[15,3,128]{2,0,1:T(8,128)S(1)}, u32[]{:S(2)}, u32[]{:S(2)}) collective-permute-start(f32[15,3,128]{2,0,1:T(8,128)S(1)} %collective-permute-done.14), channel_id=1, source_target_pairs={{0,4},{4,8},{8,12},{12,16},{16,20},{20,24},{24,28},{28,0},{1,5},{5... | collective-permute-start | bytes 69128 | tf_op jit(solution)/shard_map/ppermute | solution.py:140
  115.3 5.0 %collective-permute-start.16 = (f32[15,3,128]{2,0,1:T(8,128)S(1)}, f32[15,3,128]{2,0,1:T(8,128)S(1)}, u32[]{:S(2)}, u32[]{:S(2)}) collective-permute-start(f32[15,3,128]{2,0,1:T(8,128)S(1)} %collective-permute-done.15), channel_id=1, source_target_pairs={{0,4},{4,8},{8,12},{12,16},{16,20},{20,24},{24,28},{28,0},{1,5},{5... | collective-permute-start | bytes 69128 | tf_op jit(solution)/shard_map/ppermute | solution.py:140
  115.3 5.1 %collective-permute-start.10 = (f32[15,3,1,128]{3,0,1,2:T(8,128)S(1)}, f32[15,3,1,128]{3,0,1,2:T(8,128)S(1)}, u32[]{:S(2)}, u32[]{:S(2)}) collective-permute-start(f32[15,3,1,128]{3,0,1,2:T(8,128)S(1)} %bitcast.107), channel_id=1, source_target_pairs={{1,0},{2,1},{3,2},{0,3},{5,4},{6,5},{7,6},{4,7},{9,8},{10,9},{11,1... | collective-permute-start | bytes 69128 | tf_op jit(solution)/shard_map/ppermute | solution.py:24
  117.7 4.7 %collective-permute-start.9 = (f32[15,3,1,128]{3,0,1,2:T(8,128)S(1)}, f32[15,3,1,128]{3,0,1,2:T(8,128)S(1)}, u32[]{:S(2)}, u32[]{:S(2)}) collective-permute-start(f32[15,3,1,128]{3,0,1,2:T(8,128)S(1)} %bitcast.108), channel_id=1, source_target_pairs={{0,1},{1,2},{2,3},{3,0},{4,5},{5,6},{6,7},{7,4},{8,9},{9,10},{10,1... | collective-permute-start | bytes 69128 | tf_op jit(solution)/shard_map/ppermute | solution.py:22
  120.4 5.1 %collective-permute-start.17 = (f32[15,3,128]{2,0,1:T(8,128)S(1)}, f32[15,3,128]{2,0,1:T(8,128)S(1)}, u32[]{:S(2)}, u32[]{:S(2)}) collective-permute-start(f32[15,3,128]{2,0,1:T(8,128)S(1)} %collective-permute-done.16), channel_id=1, source_target_pairs={{0,4},{4,8},{8,12},{12,16},{16,20},{20,24},{24,28},{28,0},{1,5},{5... | collective-permute-start | bytes 69128 | tf_op jit(solution)/shard_map/ppermute | solution.py:140
  125.6 0.7 copy-start.6
  126.9 3.8 %copy-start.8 = (f32[15,3,8,128]{3,2,0,1:T(8,128)S(1)}, f32[15,3,8,128]{3,2,0,1:T(8,128)}, u32[]{:S(2)}) copy-start(f32[15,3,8,128]{3,2,0,1:T(8,128)} %reshape.346) | copy-start | bytes 552964
  133.1 1.7 copy-start.3
  133.1 1.7 copy-start.14
  133.1 1.7 copy-start.16
  134.7 0.7 copy-start.27
  134.7 0.7 copy-start.29
  134.7 0.7 copy-start.31
  134.8 0.7 copy-start.33
  135.3 2.5 %copy-start.1 = (bf16[1,1,5,384,384]{4,3,2,1,0:T(8,128)(2,1)S(1)}, bf16[1,1,5,384,384]{4,3,2,1,0:T(8,128)(2,1)}, u32[]{:S(2)}) copy-start(bf16[1,1,5,384,384]{4,3,2,1,0:T(8,128)(2,1)} %param.14) | copy-start | bytes 4423684
  135.3 2.5 %copy-start.10 = (f32[1,1,15,384]{3,2,1,0:T(8,128)S(1)}, f32[1,1,15,384]{3,2,1,0:T(8,128)}, u32[]{:S(2)}) copy-start(f32[1,1,15,384]{3,2,1,0:T(8,128)} %broadcast_in_dim_reshape_transpose_reshape_squeeze.20) | copy-start | bytes 69124
  135.3 3.2 %copy-start.5 = (bf16[1,1,384,384]{3,2,1,0:T(8,128)(2,1)S(1)}, bf16[1,1,384,384]{3,2,1,0:T(8,128)(2,1)}, u32[]{:S(2)}) copy-start(bf16[1,1,384,384]{3,2,1,0:T(8,128)(2,1)} %param.15) | copy-start | bytes 884740
  135.3 3.2 %copy-start.24 = (f32[15]{0:T(128)S(1)}, f32[15]{0:T(128)}, u32[]{:S(2)}) copy-start(f32[15]{0:T(128)} %copy-done.23) | copy-start | bytes 184
  135.3 31.0 %copy-start.12 = (f32[15,3,1,128]{3,2,1,0:T(1,128)S(1)}, f32[15,3,1,128]{3,2,1,0:T(1,128)}, u32[]{:S(2)}) copy-start(f32[15,3,1,128]{3,2,1,0:T(1,128)} %param.13) | copy-start | bytes 69124
  135.4 31.0 %copy-start.18 = (f32[384]{0:T(512)S(1)}, f32[384]{0:T(512)}, u32[]{:S(2)}) copy-start(f32[384]{0:T(512)} %copy-done.17) | copy-start | bytes 4612
  135.4 31.0 %copy-start.20 = (f32[384]{0:T(512)S(1)}, f32[384]{0:T(512)}, u32[]{:S(2)}) copy-start(f32[384]{0:T(512)} %copy-done.19) | copy-start | bytes 4612
Sparse Core Ops, SparseCore 0:
  58.2 30.9 reduce-scatter.2
  138.0 28.3 reduce-scatter.4
